TPU v7x, 128 devices: a whole 4x4x4 slice. The times are simulated.
128 devices in a mesh: req: 32 (over z, x, core), tp: 4 (over y).
Axes of the slice: x: 4, y: 4, z: 4, core: 2. Of those that a mesh axis runs over, the one named last changes fastest.
Arguments:
- tokens: bfloat16 [12288, 5120], P('req'), may hold values from -40 to 40
- w_query: bfloat16 [5120, 2560], P(None, 'tp'), may hold values from -0.125 to 0.125
- query_bias: float32 [2560], P('tp'), may hold values from -24 to 24
- w_keyval: bfloat16 [5120, 1024], P(None, 'tp'), may hold values from -0.21875 to 0.21875
- keyval_bias: float32 [1024], P('tp'), may hold values from -2.5 to 2.5
- w_out: bfloat16 [2560, 5120], P('tp'), may hold values from -0.25 to 0.25
- attn_gain: float32 [5120], replicated, may hold values from 0.25 to 1.75
- final_norm_gain: float32 [5120], replicated, may hold values from 0.25 to 1.75
- head_weight: bfloat16 [5120, 76032], P(None, ('req', 'tp')), may hold values from -0.25 to 0.25
- kv_pool: bfloat16 [851968, 4, 256], P('req', 'tp'), may hold values from -17 to 17
- cache_len: int32 [512], replicated, may hold values from 256 to 3072, as said below
Outputs:
- states: bfloat16 [12288, 5120], P('req', 'tp')
- new_kv: bfloat16 [12288, 4, 256], P('req', 'tp')
- row_norms: float32 [512], P('req')
- logit_max: float32 [512], replicated
- logits: float32 [512, 76032], P(None, ('req', 'tp'))
Inputs may be any that keep to these rules, and one draw needn't show every extreme that they name: `cache_len`: every cache holds 256 or 3072 rows. Exactly 64 requests hold 3072; requests i * 16 to i * 16 + 15 hold at most 8 of them for every i, and exactly 8 for some i, so their caches fill at most 26624 rows, and exactly 26624 for some i.
All inputs are finite; a program needn't handle non-finite values.
Results may differ from a plain program's by a relative error of at most 0.014.
Values may be sent and summed in bfloat16 or wider, within the bound.
A program may use at most 192 MiB of HBM per device.

v0:
```python
import math

import jax
import jax.numpy as jnp
from jax import lax
from jax.sharding import PartitionSpec as P

HD = 128
GROUP = 5
NEW = 24
LONG = 3072


THETA = 1000000.0
EPS = 1e-06
NEG = -1e30


def rope_rotate(vectors, positions):
    head_width = vectors.shape[-1]
    halfway = head_width // 2
    frequency = THETA ** (-(jnp.arange(halfway, dtype=jnp.float32) * (2.0 / head_width)))
    angles = positions[..., None] * frequency
    cosine = jnp.cos(angles)
    sine_part = jnp.sin(angles)
    front_part = vectors[..., :halfway]
    back_part = vectors[..., halfway:]
    return jnp.concatenate(
        [front_part * cosine - back_part * sine_part, back_part * cosine + front_part * sine_part],
        axis=-1,
    )


def online_update(state_in, scores, value_matrix):
    running_max, totals, weighted = state_in
    new_max = jnp.maximum(running_max, jnp.max(scores, axis=-1))
    rescale = jnp.exp(running_max - new_max)
    weight_matrix = jnp.exp(scores - new_max[..., None])
    totals = totals * rescale + jnp.sum(weight_matrix, axis=-1)
    weighted = weighted * rescale[..., None] + jnp.einsum(
        "amz,zav->amv",
        weight_matrix.astype(jnp.bfloat16),
        value_matrix,
        preferred_element_type=jnp.float32,
    )
    return (new_max, totals, weighted)


def attend_windows(query_rows, pool_part, leading_row, req_starts, req_lens, start_state):
    head_width = query_rows.shape[-1]
    kv_local = query_rows.shape[0]
    query_count = query_rows.shape[1]
    req_count = req_starts.shape[0]
    row_span = query_count // req_count
    part_rows = pool_part.shape[0]
    window_rows = min(LONG, part_rows)
    batch_size = math.gcd(req_count, 4)
    batch_count = req_count // batch_size

    def per_request(query_block, begin, length, state_max, state_totals, state_weighted):
        first = jnp.clip(begin - leading_row, 0, part_rows - window_rows)
        window = lax.dynamic_slice_in_dim(pool_part, first, window_rows, 0)
        row_index = leading_row + first + jnp.arange(window_rows, dtype=jnp.int32)
        inside = (row_index >= begin) & (row_index < begin + length)
        scores = jnp.einsum(
            "mjl,wml->mjw",
            query_block,
            window[..., :head_width],
            preferred_element_type=jnp.float32,
        )
        scores = jnp.where(inside[None, None, :], scores, -jnp.inf)
        return online_update(
            (state_max, state_totals, state_weighted), scores, window[..., head_width:]
        )

    def split_requests(array_in):
        moved = jnp.moveaxis(
            array_in.reshape((kv_local, req_count, row_span) + array_in.shape[2:]), 1, 0
        )
        return moved.reshape((batch_count, batch_size) + moved.shape[1:])

    def join_requests(array_in):
        merged = array_in.reshape((req_count,) + array_in.shape[2:])
        return jnp.moveaxis(merged, 0, 1).reshape((kv_local, query_count) + merged.shape[3:])

    def one_batch(inputs):
        return jax.vmap(per_request)(*inputs)

    batched = (
        split_requests(query_rows),
        req_starts.reshape(batch_count, batch_size),
        req_lens.reshape(batch_count, batch_size),
        split_requests(start_state[0]),
        split_requests(start_state[1]),
        split_requests(start_state[2]),
    )
    result = lax.map(one_batch, batched)
    return tuple((join_requests(part_state) for part_state in result))


def local(
    tokens,
    w_query,
    query_bias,
    w_keyval,
    keyval_bias,
    w_out,
    attn_gain,
    final_norm_gain,
    head_weight,
    kv_pool,
    cache_len,
):
    groups = lax.axis_size("req")
    my_group = lax.axis_index("req")
    tp_count = lax.axis_size("tp")
    tp_index = lax.axis_index("tp")
    tok_rows = tokens.shape[0]
    model_width = tokens.shape[1]
    per_group = tok_rows // NEW
    kv_local = kv_pool.shape[1]
    lens_grid = cache_len.reshape(groups, per_group)
    my_lens = lax.dynamic_slice_in_dim(lens_grid, my_group, 1, 0)[0]
    my_starts = jnp.cumsum(my_lens) - my_lens
    source = tokens.astype(jnp.float32)
    mean_square = jnp.mean(source * source, axis=1, keepdims=True)
    normed = (source / jnp.sqrt(mean_square + EPS) * attn_gain[None, :]).astype(jnp.bfloat16)
    query_raw = jnp.dot(normed, w_query, preferred_element_type=jnp.float32) + query_bias[None, :]
    keyval_raw = (
        jnp.dot(normed, w_keyval, preferred_element_type=jnp.float32) + keyval_bias[None, :]
    )
    positions = (my_lens[:, None] + jnp.arange(NEW, dtype=jnp.int32)[None, :]).astype(jnp.float32)
    query_heads = query_raw.reshape(per_group, NEW, kv_local, GROUP, HD)
    queries = (
        rope_rotate(query_heads, positions[:, :, None, None]) * (1.0 / math.sqrt(HD))
    ).astype(jnp.bfloat16)
    keyval_heads = keyval_raw.reshape(per_group, NEW, kv_local, 2, HD)
    key_new = rope_rotate(keyval_heads[:, :, :, 0, :], positions[:, :, None]).astype(jnp.bfloat16)
    value_new = keyval_heads[:, :, :, 1, :].astype(jnp.bfloat16)
    new_kv = jnp.concatenate([key_new, value_new], axis=-1).reshape(tok_rows, kv_local, 2 * HD)
    row_span = NEW * GROUP
    query_count = per_group * row_span
    query_rows = jnp.transpose(queries, (2, 0, 1, 3, 4)).reshape(kv_local, query_count, HD)
    start_state = (
        jnp.full((kv_local, query_count), NEG, jnp.float32),
        jnp.zeros((kv_local, query_count), jnp.float32),
        jnp.zeros((kv_local, query_count, HD), jnp.float32),
    )
    carry_state = attend_windows(query_rows, kv_pool, 0, my_starts, my_lens, start_state)
    key_rows = key_new.reshape(tok_rows, kv_local, HD)
    value_rows = value_new.reshape(tok_rows, kv_local, HD)
    new_scores = jnp.einsum(
        "kqd,mkd->kqm", query_rows, key_rows, preferred_element_type=jnp.float32
    )
    query_token = jnp.arange(query_count, dtype=jnp.int32) // GROUP
    key_token = jnp.arange(tok_rows, dtype=jnp.int32)
    allowed = (query_token[:, None] // NEW == key_token[None, :] // NEW) & (
        key_token[None, :] <= query_token[:, None]
    )
    new_scores = jnp.where(allowed[None], new_scores, -jnp.inf)
    carry_state = online_update(carry_state, new_scores, value_rows)
    attention = (carry_state[2] / carry_state[1][..., None]).astype(jnp.bfloat16)
    attention = jnp.transpose(
        attention.reshape(kv_local, per_group, NEW, GROUP, HD), (1, 2, 0, 3, 4)
    ).reshape(tok_rows, kv_local * GROUP * HD)
    partial_value = jnp.dot(attention, w_out, preferred_element_type=jnp.float32)
    width_local = model_width // tp_count
    summed = lax.psum(partial_value.astype(jnp.bfloat16), "tp").astype(jnp.float32)
    states_full = (source + summed).astype(jnp.bfloat16)
    states = lax.dynamic_slice_in_dim(states_full, tp_index * width_local, width_local, 1)
    last_rows = states_full.reshape(per_group, NEW, model_width)[:, NEW - 1, :].astype(jnp.float32)
    row_norms = jnp.sqrt(jnp.mean(last_rows * last_rows, axis=1) + EPS)
    final_rows = (last_rows / row_norms[:, None] * final_norm_gain[None, :]).astype(jnp.bfloat16)
    logits = jnp.dot(
        lax.all_gather(final_rows, "req", axis=0, tiled=True),
        head_weight,
        preferred_element_type=jnp.float32,
    )
    logit_max = lax.pmax(jnp.max(logits, axis=1), ("req", "tp"))
    return (states, new_kv, row_norms, logit_max, logits)


def solution(mesh):
    return jax.shard_map(
        local,
        mesh=mesh,
        in_specs=(
            P("req", None),
            P(None, "tp"),
            P("tp"),
            P(None, "tp"),
            P("tp"),
            P("tp", None),
            P(),
            P(),
            P(None, ("req", "tp")),
            P("req", "tp", None),
            P(),
        ),
        out_specs=(P("req", "tp"), P("req", "tp", None), P("req"), P(), P(None, ("req", "tp"))),
        check_vma=False,
    )
```

profile of v0, /device:TPU:1, one launch (start us, length us, event | category | flops | bytes accessed | tf_op | source)
XLA Modules:
  0.0 364.9 jit_solution(11805179985593253152)
XLA Ops:
  7.3 3.1 fusion.27
  10.7 3.6 fusion.29
  16.1 4.2 %convolution_add_fusion.1 = f32[384,640]{1,0:T(8,128)} fusion(bf16[384,5120]{1,0:T(8,128)(2,1)S(1)} %fusion.29, bf16[5120,640]{1,0:T(8,128)(2,1)S(1)} %copy-done.12, f32[640]{0:T(1024)S(1)} %copy-done.13), kind=kOutput, calls=%fused_computation.58 | convolution fusion | flops 2516828160 | bytes 11471360 | tf_op jit(solution)/shard_map/dot_general | solution.py:128
  23.5 4.2 %multiply_subtract_fusion = (f32[16,24,1,5,64]{4,3,1,0,2:T(8,128)}, f32[16,24,1,5,64]{4,3,1,0,2:T(8,128)}) fusion(f32[16,24,1,5,128]{4,3,1,0,2:T(8,128)} %reshape.555, f32[16,24,64]{2,1,0:T(8,128)S(1)} %get-tuple-element.120, f32[16,24,64]{2,1,0:T(8,128)S(1)} %get-tuple-element.119), kind=kLoop, calls=%fused_computation.56 | loop fusion | flops 737280 | bytes 2162688 | tf_op jit(solution)/shard_map/sub | solution.py:29
  38.9 3.3 convolution_add_fusion.2
  45.7 81.0 %while.17 = (s32[]{:T(128)}, f32[4,4,1,120]{3,1,2,0:T(4,128)S(1)}, f32[4,4,1,120]{3,1,2,0:T(4,128)S(1)}, f32[4,4,1,120,128]{4,3,1,2,0:T(8,128)}, s32[4,4]{1,0:T(...) while((s32[]{:T(128)}, f32[4,4,1,120]{3,1,2,0:T(4,128)S(1)}, ...), condition=%wide.region_5.6_spmd, body=%wide.region_2.5_spmd.sunk | while | flops 766884224 | bytes 52985684 | solution.py:97
  46.1 12.2 %while.18 = (s32[]{:T(128)}, bf16[26624,1,256]{2,0,1:T(8,128)(2,1)}, s32[4,3]{1,0:T(4,128)S(1)}, bf16[4,3072,1,256]{3,1,2,0:T(8,128)(2,1)}, s32[]{:T(128)}) while((s32[]{:T(128)}, bf16[26624,1,256]{2,0,1:T(8,128)(2,1)}, s32[4,3]{1,0:T(4,128)S(1)}, bf16[4,3072,1,256]{3,1,2,0:T(8,128)(2,1)}, s32[]{:T(128)}) %tuple.62), condition=%wide.while_cond, body=%wide.while_body.sunk | while | flops 2 | bytes 3145833 | solution.py:62
  46.1 3.2 bitcast_dynamic-update-slice_fusion.3
  49.3 3.0 bitcast_dynamic-update-slice_fusion.3
  52.3 3.0 bitcast_dynamic-update-slice_fusion.3
  55.3 3.0 bitcast_dynamic-update-slice_fusion.3
  58.3 4.2 %select_reduce_fusion.2 = (f32[4,120]{1,0:T(4,128)S(1)}, f32[4,120,3072]{2,1,0:T(8,128)S(1)}) fusion(pred[4,3072]{1,0:T(4,128)(4,1)S(1)} %fusion.90, bf16[4,3072,1,256]{3,1,0,2:T(8,128)(2,1)} %bitcast.118, bf16[1,4,1,120,128]{4,1,0,3,2:T(4,128)(2,1)S(1)} %constant_dynamic-slice_fusion.8), kind=kOutput, calls=%fused_computation.3.clone.1 | convolution fusion | flops 380436000 | bytes 9181056 | tf_op jit(solution)/shard_map/while/body/eval_jaxpr/vmap(mjl,wml->mjw)/dot_general | solution.py:65
  66.4 12.1 %while.18 = (s32[]{:T(128)}, bf16[26624,1,256]{2,0,1:T(8,128)(2,1)}, s32[4,3]{1,0:T(4,128)S(1)}, bf16[4,3072,1,256]{3,1,2,0:T(8,128)(2,1)}, s32[]{:T(128)}) while((s32[]{:T(128)}, bf16[26624,1,256]{2,0,1:T(8,128)(2,1)}, s32[4,3]{1,0:T(4,128)S(1)}, bf16[4,3072,1,256]{3,1,2,0:T(8,128)(2,1)}, s32[]{:T(128)}) %tuple.62), condition=%wide.while_cond, body=%wide.while_body.sunk | while | flops 2 | bytes 3145833 | solution.py:62
  66.4 3.0 bitcast_dynamic-update-slice_fusion.3
  69.4 3.0 bitcast_dynamic-update-slice_fusion.3
  72.4 3.0 bitcast_dynamic-update-slice_fusion.3
  75.4 3.0 bitcast_dynamic-update-slice_fusion.3
  78.4 4.2 %select_reduce_fusion.2 = (f32[4,120]{1,0:T(4,128)S(1)}, f32[4,120,3072]{2,1,0:T(8,128)S(1)}) fusion(pred[4,3072]{1,0:T(4,128)(4,1)S(1)} %fusion.90, bf16[4,3072,1,256]{3,1,0,2:T(8,128)(2,1)} %bitcast.118, bf16[1,4,1,120,128]{4,1,0,3,2:T(4,128)(2,1)S(1)} %constant_dynamic-slice_fusion.8), kind=kOutput, calls=%fused_computation.3.clone.1 | convolution fusion | flops 380436000 | bytes 9181056 | tf_op jit(solution)/shard_map/while/body/eval_jaxpr/vmap(mjl,wml->mjw)/dot_general | solution.py:65
  86.5 12.1 %while.18 = (s32[]{:T(128)}, bf16[26624,1,256]{2,0,1:T(8,128)(2,1)}, s32[4,3]{1,0:T(4,128)S(1)}, bf16[4,3072,1,256]{3,1,2,0:T(8,128)(2,1)}, s32[]{:T(128)}) while((s32[]{:T(128)}, bf16[26624,1,256]{2,0,1:T(8,128)(2,1)}, s32[4,3]{1,0:T(4,128)S(1)}, bf16[4,3072,1,256]{3,1,2,0:T(8,128)(2,1)}, s32[]{:T(128)}) %tuple.62), condition=%wide.while_cond, body=%wide.while_body.sunk | while | flops 2 | bytes 3145833 | solution.py:62
  86.5 3.0 bitcast_dynamic-update-slice_fusion.3
  95.6 3.0 bitcast_dynamic-update-slice_fusion.3
  98.6 4.2 %select_reduce_fusion.2 = (f32[4,120]{1,0:T(4,128)S(1)}, f32[4,120,3072]{2,1,0:T(8,128)S(1)}) fusion(pred[4,3072]{1,0:T(4,128)(4,1)S(1)} %fusion.90, bf16[4,3072,1,256]{3,1,0,2:T(8,128)(2,1)} %bitcast.118, bf16[1,4,1,120,128]{4,1,0,3,2:T(4,128)(2,1)S(1)} %constant_dynamic-slice_fusion.8), kind=kOutput, calls=%fused_computation.3.clone.1 | convolution fusion | flops 380436000 | bytes 9181056 | tf_op jit(solution)/shard_map/while/body/eval_jaxpr/vmap(mjl,wml->mjw)/dot_general | solution.py:65
  106.7 12.1 %while.18 = (s32[]{:T(128)}, bf16[26624,1,256]{2,0,1:T(8,128)(2,1)}, s32[4,3]{1,0:T(4,128)S(1)}, bf16[4,3072,1,256]{3,1,2,0:T(8,128)(2,1)}, s32[]{:T(128)}) while((s32[]{:T(128)}, bf16[26624,1,256]{2,0,1:T(8,128)(2,1)}, s32[4,3]{1,0:T(4,128)S(1)}, bf16[4,3072,1,256]{3,1,2,0:T(8,128)(2,1)}, s32[]{:T(128)}) %tuple.62), condition=%wide.while_cond, body=%wide.while_body.sunk | while | flops 2 | bytes 3145833 | solution.py:62
  106.7 3.0 bitcast_dynamic-update-slice_fusion.3
  115.7 3.0 bitcast_dynamic-update-slice_fusion.3
  118.7 4.2 %select_reduce_fusion.2 = (f32[4,120]{1,0:T(4,128)S(1)}, f32[4,120,3072]{2,1,0:T(8,128)S(1)}) fusion(pred[4,3072]{1,0:T(4,128)(4,1)S(1)} %fusion.90, bf16[4,3072,1,256]{3,1,0,2:T(8,128)(2,1)} %bitcast.118, bf16[1,4,1,120,128]{4,1,0,3,2:T(4,128)(2,1)S(1)} %constant_dynamic-slice_fusion.8), kind=kOutput, calls=%fused_computation.3.clone.1 | convolution fusion | flops 380436000 | bytes 9181056 | tf_op jit(solution)/shard_map/while/body/eval_jaxpr/vmap(mjl,wml->mjw)/dot_general | solution.py:65
  129.9 7.6 %convolution_convert_fusion = bf16[384,5120]{1,0:T(8,128)(2,1)} fusion(bf16[384,640]{1,0:T(8,128)(2,1)S(1)} %reshape_transpose_reshape.16, bf16[640,5120]{1,0:T(8,128)(2,1)} %param.18), kind=kOutput, calls=%fused_computation.45 | convolution fusion | flops 2518548480 | bytes 10977280 | tf_op jit(solution)/shard_map/dot_general | solution.py:166
  137.5 91.6 %all-reduce.3.cloned.1.call-done = bf16[384,5120]{1,0:T(8,128)(2,1)} async-done(((bf16[384,5120]{1,0:T(8,128)(2,1)}), bf16[384,5120]{1,0:T(8,128)(2,1)}) %all-reduce.3.cloned.1.call-update) | async-done | bytes 3932176 | tf_op jit(solution)/shard_map/psum | solution.py:168
  229.2 4.8 %fusion.30 = bf16[384,5120]{1,0:T(8,128)(2,1)S(1)} fusion(bf16[384,5120]{1,0:T(8,128)(2,1)} %param.13, bf16[384,5120]{1,0:T(8,128)(2,1)} %all-reduce.3.cloned.1.call-done), kind=kLoop, calls=%fused_computation.44 | loop fusion | flops 7864320 | bytes 11796480 | tf_op jit(solution)/shard_map/convert_element_type | solution.py:169
  240.2 44.9 %all-gather.2.cloned.1.call-done = bf16[512,5120]{1,0:T(8,128)(2,1)} async-done(((bf16[16,5120]{1,0:T(8,128)(2,1)}), bf16[512,5120]{1,0:T(8,128)(2,1)}) %all-gather.2.cloned.1.call-update) | async-done | bytes 5242896 | tf_op jit(solution)/shard_map/all_gather | solution.py:175
  285.1 8.8 %fusion.72 = (f32[512]{0:T(512)S(1)}, f32[512,594]{0,1:T(8,128)}) fusion(bf16[512,5120]{1,0:T(8,128)(2,1)} %all-gather.2.cloned.1.call-done, bf16[5120,594]{0,1:T(8,128)(2,1)} %param.21), kind=kOutput, calls=%fused_computation.122 | convolution fusion | flops 3114574336 | bytes 12544000 | tf_op jit(solution)/shard_map/dot_general | solution.py:174
  293.9 64.1 %pmax.7 = f32[512]{0:T(512)} all-reduce(f32[512]{0:T(512)S(1)} %get-tuple-element.123), channel_id=1, replica_groups=mesh['req'=32,'tp'=4] {'req','tp'}, use_global_device_ids=true, to_apply=%region_11.12 | all-reduce | flops 512 | bytes 4096 | tf_op jit(solution)/shard_map/pmax | solution.py:179
  (150 shorter events, 56.6 us)
Async XLA Ops:
  7.2 31.7 %copy-start = (bf16[5120,256]{1,0:T(8,128)(2,1)S(1)}, bf16[5120,256]{1,0:T(8,128)(2,1)}, u32[]{:S(2)}) copy-start(bf16[5120,256]{1,0:T(8,128)(2,1)} %param.16) | copy-start | bytes 7864324
  7.2 3.3 copy-start.10
  7.2 3.5 copy-start.8
  7.2 222.0 %all-reduce.3.cloned.1.call-start = ((), (), s32[]{:S(2)}) async-start(), calls=%async_computation | async-start | bytes 7864320 | tf_op jit(solution)/shard_map/psum | solution.py:168
  10.6 5.5 %copy-start.12 = (bf16[5120,640]{1,0:T(8,128)(2,1)S(1)}, bf16[5120,640]{1,0:T(8,128)(2,1)}, u32[]{:S(2)}) copy-start(bf16[5120,640]{1,0:T(8,128)(2,1)} %param.14) | copy-start | bytes 19660804
  10.7 5.5 %copy-start.13 = (f32[640]{0:T(1024)S(1)}, f32[640]{0:T(1024)}, u32[]{:S(2)}) copy-start(f32[640]{0:T(1024)} %param.15) | copy-start | bytes 7684
  14.2 1.9 copy-start.4
  30.1 8.8 %copy-start.14 = (f32[256]{0:T(256)S(1)}, f32[256]{0:T(256)}, u32[]{:S(2)}) copy-start(f32[256]{0:T(256)} %param.17) | copy-start | bytes 3076
  45.7 81.2 %copy-start.5 = (f32[1920,64]{1,0:T(8,128)S(1)}, f32[1920,64]{1,0:T(8,128)}, u32[]{:S(2)}) copy-start(f32[1920,64]{1,0:T(8,128)} %concatenate.59) | copy-start | bytes 1474564
  45.7 81.2 %copy-start.6 = (f32[1920,64]{1,0:T(8,128)S(1)}, f32[1920,64]{1,0:T(8,128)}, u32[]{:S(2)}) copy-start(f32[1920,64]{1,0:T(8,128)} %concatenate.60) | copy-start | bytes 1474564
  58.3 4.2 %copy-start.2 = (bf16[4,3072,1,256]{3,1,2,0:T(8,128)(2,1)S(1)}, bf16[4,3072,1,256]{3,1,2,0:T(8,128)(2,1)}, u32[]{:S(2)}) copy-start(bf16[4,3072,1,256]{3,1,2,0:T(8,128)(2,1)} %get-tuple-element.216) | copy-start | bytes 18874372 | tf_op jit(solution)/shard_map/while
  78.4 4.2 %copy-start.2 = (bf16[4,3072,1,256]{3,1,2,0:T(8,128)(2,1)S(1)}, bf16[4,3072,1,256]{3,1,2,0:T(8,128)(2,1)}, u32[]{:S(2)}) copy-start(bf16[4,3072,1,256]{3,1,2,0:T(8,128)(2,1)} %get-tuple-element.216) | copy-start | bytes 18874372 | tf_op jit(solution)/shard_map/while
  98.6 4.2 %copy-start.2 = (bf16[4,3072,1,256]{3,1,2,0:T(8,128)(2,1)S(1)}, bf16[4,3072,1,256]{3,1,2,0:T(8,128)(2,1)}, u32[]{:S(2)}) copy-start(bf16[4,3072,1,256]{3,1,2,0:T(8,128)(2,1)} %get-tuple-element.216) | copy-start | bytes 18874372 | tf_op jit(solution)/shard_map/while
  118.7 4.2 %copy-start.2 = (bf16[4,3072,1,256]{3,1,2,0:T(8,128)(2,1)S(1)}, bf16[4,3072,1,256]{3,1,2,0:T(8,128)(2,1)}, u32[]{:S(2)}) copy-start(bf16[4,3072,1,256]{3,1,2,0:T(8,128)(2,1)} %get-tuple-element.216) | copy-start | bytes 18874372 | tf_op jit(solution)/shard_map/while
  126.9 1.5 copy-start.7
  137.5 98.9 %copy-start.9 = (f32[5120]{0:T(1024)S(1)}, f32[5120]{0:T(1024)}, u32[]{:S(2)}) copy-start(f32[5120]{0:T(1024)} %param.20) | copy-start | bytes 61444
  137.5 147.6 %all-gather.2.cloned.1.call-start = ((), (), s32[]{:S(2)}) async-start(), calls=%async_computation.1 | async-start | bytes 5406720 | tf_op jit(solution)/shard_map/all_gather | solution.py:175
  234.0 1.9 copy-start.3
  236.4 57.5 %copy-start.11 = (f32[16]{0:T(128)}, f32[16]{0:T(128)S(1)}, u32[]{:S(2)}) copy-start(f32[16]{0:T(128)S(1)} %add_sqrt_fusion.1) | copy-start | bytes 196
  285.1 73.0 %copy-start.1 = (bf16[5120,256]{1,0:T(8,128)(2,1)S(1)}, bf16[5120,256]{1,0:T(8,128)(2,1)}, u32[]{:S(2)}) copy-start(bf16[5120,256]{1,0:T(8,128)(2,1)} %param.16) | copy-start | bytes 7864324
Sparse Core Ops, SparseCore 0:
  137.6 91.5 all-reduce.2
  237.3 47.7 all-gather.1
where the time goes:
time: 366 us; the launch traced here: 365 us
  waiting for transfers between devices  137 us (37%)
  local copies, waits for them, and re-layouts  69.7 us (19%)
  blocking collectives  64.1 us (18%)
  matrix products  51.4 us (14%)
  other arithmetic  28.1 us (8%)
  between operations  14.4 us (4%)
    psum x1, waiting for transfers between devices, local(): lax.psum(partial_value.astype(jnp.bfloat16), 'tp').astype(jnp.float32)  91.6 us
    pmax x1, blocking collectives, local(): logit_max = lax.pmax(jnp.max(logits, axis=1), ('req', 'tp'))  64.1 us
    gather x32, local copies, waits for them, and re-layouts  48.3 us
    all_gather x1, waiting for transfers between devices, local(): lax.all_gather(final_rows, 'req', axis=0, tiled=True)  44.9 us
    dot_general x4, matrix products, per_request(): jnp.einsum('mjl,wml->mjw', query_block, window[..., :head_width], preferr...  16.9 us
    dot_general x5, matrix products, online_update(): jnp.einsum('amz,zav->amv', weight_matrix.astype(jnp.bfloat16), value_matr...  9.56 us
    dot_general x1, matrix products, local(): jnp.dot(lax.all_gather(final_rows, 'req', axis=0, tiled=True), head_weigh...  8.84 us
    dot_general x1, matrix products, local(): jnp.dot(attention, w_out, preferred_element_type=jnp.float32)  7.58 us
  transfers between devices with their start and end apart: 2, of which 2 were waited for; matrix products, arithmetic and copies ran while one was open for 1% of the time, Pallas kernels for 0%

commit v1 on v0

v1 whole, which is shorter than its diff:
```python
import math

import jax
import jax.numpy as jnp
from jax import lax
from jax.experimental import pallas as pl
from jax.experimental.pallas import tpu as pltpu
from jax.sharding import PartitionSpec as P

HD = 128
GROUP = 5
NEW = 24
SHORT = 256
LONG = 3072


THETA = 1000000.0
EPS = 1e-06


def attention_kernel(
    starts_ref, lens_ref, query_ref, keyval_ref, cos_ref, sin_ref, pool_ref, out_ref, new_ref, cache, sems
):
    requests = query_ref.shape[0]

    def fetch(r, rows):
        begin = pl.multiple_of(starts_ref[r], SHORT)
        window = pl.ds(begin, rows)
        return pltpu.make_async_copy(pool_ref.at[window], cache.at[window], sems.at[r])

    def start_copy(r, carry):
        @pl.when(lens_ref[r] == LONG)
        def _():
            fetch(r, LONG).start()

        @pl.when(lens_ref[r] != LONG)
        def _():
            fetch(r, SHORT).start()

        return carry

    lax.fori_loop(0, requests, start_copy, 0)

    def attend(r, rows):
        cosine = cos_ref[r]
        sine = sin_ref[r]

        def rotate(v):
            return v * cosine + pltpu.roll(v, HD // 2, 1) * sine

        heads = [
            rotate(query_ref[r, :, g * HD : (g + 1) * HD]) * (1.0 / math.sqrt(HD))
            for g in range(GROUP)
        ]
        queries = jnp.concatenate(heads, axis=0).astype(jnp.bfloat16)
        key_new = rotate(keyval_ref[r, :, :HD])
        value_new = keyval_ref[r, :, HD:]
        new_ref[r, :, :HD] = key_new
        new_ref[r, :, HD:] = value_new
        pad = jnp.zeros((HD - NEW, HD), jnp.float32)
        key_pad = jnp.concatenate([key_new, pad], axis=0).astype(jnp.bfloat16)
        value_pad = jnp.concatenate([value_new, pad], axis=0).astype(jnp.bfloat16)
        contract = (((1,), (1,)), ((), ()))
        new_scores = lax.dot_general(queries, key_pad, contract, preferred_element_type=jnp.float32)
        token = jnp.concatenate(
            [lax.broadcasted_iota(jnp.int32, (NEW, HD), 0)] * GROUP, axis=0
        )
        column = lax.broadcasted_iota(jnp.int32, (GROUP * NEW, HD), 1)
        new_scores = jnp.where(column <= token, new_scores, -jnp.inf)
        fetch(r, rows).wait()
        window = pl.ds(pl.multiple_of(starts_ref[r], SHORT), rows)
        scores = lax.dot_general(
            queries, cache[window, :HD], contract, preferred_element_type=jnp.float32
        )
        row_max = jnp.maximum(
            jnp.max(scores, axis=1, keepdims=True), jnp.max(new_scores, axis=1, keepdims=True)
        )
        exps = jnp.exp(scores - row_max)
        new_exps = jnp.exp(new_scores - row_max)
        totals = jnp.sum(exps, axis=1, keepdims=True) + jnp.sum(new_exps, axis=1, keepdims=True)
        mixed = jnp.dot(
            exps.astype(jnp.bfloat16), cache[window, HD:], preferred_element_type=jnp.float32
        ) + jnp.dot(new_exps.astype(jnp.bfloat16), value_pad, preferred_element_type=jnp.float32)
        result = mixed / totals
        for g in range(GROUP):
            out_ref[r, :, g * HD : (g + 1) * HD] = result[g * NEW : (g + 1) * NEW, :]

    def step(r, carry):
        @pl.when(lens_ref[r] == LONG)
        def _():
            attend(r, LONG)

        @pl.when(lens_ref[r] != LONG)
        def _():
            attend(r, SHORT)

        return carry

    lax.fori_loop(0, requests, step, 0)


def attend_all(starts, lens, query_raw, keyval_raw, cosine, sine, pool):
    requests = lens.shape[0]
    smem = pl.BlockSpec(memory_space=pltpu.SMEM)
    vmem = pl.BlockSpec(memory_space=pltpu.VMEM)
    return pl.pallas_call(
        attention_kernel,
        out_shape=(
            jax.ShapeDtypeStruct(query_raw.shape, jnp.float32),
            jax.ShapeDtypeStruct(keyval_raw.shape, jnp.float32),
        ),
        in_specs=[smem, smem, vmem, vmem, vmem, vmem, pl.BlockSpec(memory_space=pl.ANY)],
        out_specs=(vmem, vmem),
        scratch_shapes=[
            pltpu.VMEM(pool.shape, pool.dtype),
            pltpu.SemaphoreType.DMA((requests,)),
        ],
        compiler_params=pltpu.CompilerParams(vmem_limit_bytes=48 * 1024 * 1024),
    )(starts, lens, query_raw, keyval_raw, cosine, sine, pool)


def local(
    tokens,
    w_query,
    query_bias,
    w_keyval,
    keyval_bias,
    w_out,
    attn_gain,
    final_norm_gain,
    head_weight,
    kv_pool,
    cache_len,
):
    groups = lax.axis_size("req")
    my_group = lax.axis_index("req")
    tp_count = lax.axis_size("tp")
    tp_index = lax.axis_index("tp")
    tok_rows = tokens.shape[0]
    model_width = tokens.shape[1]
    per_group = tok_rows // NEW
    kv_local = kv_pool.shape[1]
    lens_grid = cache_len.reshape(groups, per_group)
    my_lens = lax.dynamic_slice_in_dim(lens_grid, my_group, 1, 0)[0]
    my_starts = jnp.cumsum(my_lens) - my_lens
    source = tokens.astype(jnp.float32)
    mean_square = jnp.mean(source * source, axis=1, keepdims=True)
    normed = (source / jnp.sqrt(mean_square + EPS) * attn_gain[None, :]).astype(jnp.bfloat16)
    query_raw = jnp.dot(normed, w_query, preferred_element_type=jnp.float32) + query_bias[None, :]
    keyval_raw = (
        jnp.dot(normed, w_keyval, preferred_element_type=jnp.float32) + keyval_bias[None, :]
    )
    positions = (my_lens[:, None] + jnp.arange(NEW, dtype=jnp.int32)[None, :]).astype(jnp.float32)
    half = HD // 2
    frequency = THETA ** (-(jnp.arange(half, dtype=jnp.float32) * (2.0 / HD)))
    angles = positions[..., None] * frequency
    cosine = jnp.cos(angles)
    sine = jnp.sin(angles)
    mixed, new_rows = attend_all(
        my_starts.astype(jnp.int32),
        my_lens.astype(jnp.int32),
        query_raw.reshape(per_group, NEW, GROUP * HD),
        keyval_raw.reshape(per_group, NEW, 2 * HD),
        jnp.concatenate([cosine, cosine], axis=-1),
        jnp.concatenate([-sine, sine], axis=-1),
        kv_pool.reshape(kv_pool.shape[0], 2 * HD),
    )
    new_kv = new_rows.astype(jnp.bfloat16).reshape(tok_rows, kv_local, 2 * HD)
    attention = mixed.astype(jnp.bfloat16).reshape(tok_rows, GROUP * HD)
    partial_value = jnp.dot(attention, w_out, preferred_element_type=jnp.float32)
    width_local = model_width // tp_count
    summed = lax.psum_scatter(
        partial_value.astype(jnp.bfloat16), "tp", scatter_dimension=1, tiled=True
    ).astype(jnp.float32)
    source_part = lax.dynamic_slice_in_dim(tokens, tp_index * width_local, width_local, 1)
    states = (source_part.astype(jnp.float32) + summed).astype(jnp.bfloat16)
    last_part = states.reshape(per_group, NEW, width_local)[:, NEW - 1, :]
    gathered = lax.all_gather(last_part, ("req", "tp"), axis=0, tiled=False)
    last_rows = (
        jnp.transpose(gathered.reshape(groups, tp_count, per_group, width_local), (0, 2, 1, 3))
        .reshape(groups * per_group, model_width)
        .astype(jnp.float32)
    )
    all_norms = jnp.sqrt(jnp.mean(last_rows * last_rows, axis=1) + EPS)
    row_norms = lax.dynamic_slice_in_dim(all_norms, my_group * per_group, per_group, 0)
    final_rows = (last_rows / all_norms[:, None] * final_norm_gain[None, :]).astype(jnp.bfloat16)
    logits = jnp.dot(final_rows, head_weight, preferred_element_type=jnp.float32)
    local_max = jnp.max(logits, axis=1)
    logit_max = jnp.max(lax.all_gather(local_max, ("req", "tp"), axis=0, tiled=False), axis=0)
    return (states, new_kv, row_norms, logit_max, logits)


def solution(mesh):
    return jax.shard_map(
        local,
        mesh=mesh,
        in_specs=(
            P("req", None),
            P(None, "tp"),
            P("tp"),
            P(None, "tp"),
            P("tp"),
            P("tp", None),
            P(),
            P(),
            P(None, ("req", "tp")),
            P("req", "tp", None),
            P(),
        ),
        out_specs=(P("req", "tp"), P("req", "tp", None), P("req"), P(), P(None, ("req", "tp"))),
        check_vma=False,
    )
```

time: 366 us -> 266 us (0.73)
  local copies, waits for them, and re-layouts: 69.7 us -> 25.7 us
  matrix products: 51.4 us -> 16.6 us
  waiting for transfers between devices: 137 us -> 119 us
  Pallas kernels: 0 us -> 12.5 us
  blocking collectives: 64.1 us -> 55.1 us
  other arithmetic: 28.1 us -> 22 us
    psum x1 -> x0, waiting for transfers between devices: 91.6 us -> none  [local(): lax.psum(partial_value.astype(jnp.bfloat16), 'tp').astype(jnp.float32)]
    pmax x1 -> x0, blocking collectives: 64.1 us -> none  [local(): logit_max = lax.pmax(jnp.max(logits, axis=1), ('req', 'tp'))]
    all_gather x0 -> x1, blocking collectives: none -> 55.1 us  [local(): lax.all_gather(local_max, ('req', 'tp'), axis=0, tiled=False)]
    reduce_scatter x0 -> x1, waiting for transfers between devices: none -> 51.3 us  [local(): lax.psum_scatter(partial_value.astype(jnp.bfloat16), 'tp', scatter_dimens...]
    gather x32 -> x0, local copies, waits for them, and re-layouts: 48.3 us -> none
    dot_general x11 -> x1, matrix products: 36.4 us -> 7.38 us  [local(): jnp.dot(final_rows, head_weight, preferred_element_type=jnp.float32)]
    all_gather x1, waiting for transfers between devices: 44.9 us -> 67.9 us  [local(): gathered = lax.all_gather(last_part, ('req', 'tp'), axis=0, tiled=False)]
    convert_element_type x0 -> x1, local copies, waits for them, and re-layouts: none -> 16.7 us  [local(): last_rows = jnp.transpose(gathered.reshape(groups, tp_count, per_group, w...]
  transfers between devices with their start and end apart: 2 -> 2, of which waited for: 2 -> 2; matrix products, arithmetic and copies ran while one was open for 1% -> 0% of each run, Pallas kernels for 0% -> 0%
where the time goes in v1:
time: 266 us
  waiting for transfers between devices  119 us (45%)
  blocking collectives  55.1 us (21%)
  local copies, waits for them, and re-layouts  25.7 us (10%)
  other arithmetic  22 us (8%)
  matrix products  16.6 us (6%)
  between operations  14.3 us (5%)
  Pallas kernels  12.5 us (5%)
    all_gather x1, waiting for transfers between devices, local(): gathered = lax.all_gather(last_part, ('req', 'tp'), axis=0, tiled=False)  67.9 us
    all_gather x1, blocking collectives, local(): lax.all_gather(local_max, ('req', 'tp'), axis=0, tiled=False)  55.1 us
    reduce_scatter x1, waiting for transfers between devices, local(): lax.psum_scatter(partial_value.astype(jnp.bfloat16), 'tp', scatter_dimens...  51.3 us
    convert_element_type x1, local copies, waits for them, and re-layouts, local(): last_rows = jnp.transpose(gathered.reshape(groups, tp_count, per_group, w...  16.7 us
    pallas_call x1, Pallas kernels, attend_all(): pl.pallas_call(attention_kernel, out_shape=(jax.ShapeDtypeStruct(query_ra...  12.5 us
    dot_general x1, matrix products, local(): jnp.dot(final_rows, head_weight, preferred_element_type=jnp.float32)  7.38 us
    unnamed x22, local copies, waits for them, and re-layouts  7.29 us
    convert_element_type x1, other arithmetic, local(): last_rows = jnp.transpose(gathered.reshape(groups, tp_count, per_group, w...  7.28 us
  transfers between devices with their start and end apart: 2, of which 2 were waited for; matrix products, arithmetic and copies ran while one was open for 0% of the time, Pallas kernels for 0%

profile of v1, /device:TPU:1, one launch (start us, length us, event | category | flops | bytes accessed | tf_op | source)
XLA Modules:
  0.0 265.7 jit_solution(18118026252763157307)
XLA Ops:
  7.2 0.0 reduce-scatter.2.cloned.1.call-start
  7.3 3.1 %fusion = f32[384]{0:T(512)S(1)} fusion(bf16[384,5120]{1,0:T(8,128)(2,1)} %param.11), kind=kLoop, calls=%fused_computation.4 | loop fusion | flops 5897856 | bytes 3933696 | tf_op jit(solution)/shard_map/reduce_sum | solution.py:147
  10.4 0.8 reshape.124
  11.2 0.1 copy.21
  11.3 0.1 reduce.7
  11.4 0.1 add_convert_fusion.1
  11.5 0.8 fusion.4
  12.3 3.6 %fusion.2 = bf16[384,5120]{1,0:T(8,128)(2,1)S(1)} fusion(bf16[384,5120]{1,0:T(8,128)(2,1)} %param.11, f32[5120]{0:T(1024)} %param.17, f32[384]{0:T(512)S(1)} %add_sqrt_fusion.1), kind=kLoop, calls=%fused_computation.6 | loop fusion | flops 7864320 | bytes 7886336 | tf_op jit(solution)/shard_map/convert_element_type | solution.py:148
  15.9 1.2 convolution_add_fusion.1
  17.2 3.2 %convolution_add_fusion = f32[384,640]{1,0:T(8,128)S(1)} fusion(bf16[384,5120]{1,0:T(8,128)(2,1)S(1)} %fusion.2, bf16[5120,640]{1,0:T(8,128)(2,1)S(1)} %bitcast.36, f32[640]{0:T(1024)S(1)} %copy-done.4), kind=kOutput, calls=%fused_computation.10 | convolution fusion | flops 2516828160 | bytes 11471360 | tf_op jit(solution)/shard_map/dot_general | solution.py:149
  20.4 0.2 pad_maximum_fusion
  20.6 12.5 %shard_map.146 = (f32[16,24,640]{2,1,0:T(8,128)S(1)}, f32[16,24,256]{2,1,0:T(8,128)S(1)}) custom-call(s32[16]{0:T(128)S(1)} %get-tuple-element.9.starts_ref, s32[16]{0:T(128)S(1)} %get-tuple-element.10.lens_ref, f32[16,24,640]{2,1,0:T(8,128)S(1)} %bitcast.25, f32[16,24,256]{2,1,0:T(8,128)S(1)} %bitcast.26, f32[16,24,128]{2,1,0:T(8,128)S(1)} %get-tuple-element.16.cos_ref, ...), custom_call_target="tpu_custom_call" | custom-call | tf_op jit(solution)/shard_map/pallas_call | solution.py:106
  33.1 0.1 convert_element_type.55
  33.2 4.7 %convolution_convert_fusion = bf16[384,5120]{1,0:T(8,128)(2,1)} fusion(bf16[384,640]{1,0:T(8,128)(2,1)S(1)} %bitcast.32, bf16[640,5120]{1,0:T(8,128)(2,1)S(1)} %bitcast.38), kind=kOutput, calls=%fused_computation.7 | convolution fusion | flops 2518548480 | bytes 10977280 | tf_op jit(solution)/shard_map/dot_general | solution.py:170
  38.0 0.0 reduce-scatter.2.cloned.1.call-update
  38.0 0.2 all-gather.5.cloned.1.call-start
  38.2 51.3 %reduce-scatter.2.cloned.1.call-done = bf16[384,1280]{1,0:T(8,128)(2,1)} async-done(((bf16[384,5120]{1,0:T(8,128)(2,1)}), bf16[384,1280]{1,0:T(8,128)(2,1)}) %reduce-scatter.2.cloned.1.call-update) | async-done | bytes 983056 | tf_op jit(solution)/shard_map/reduce_scatter | solution.py:172
  89.5 1.7 add_convert_fusion
  91.3 0.1 slice.4
  91.4 0.7 copy.24
  92.1 0.7 convert_element_type.59
  92.8 67.9 %all-gather.5.cloned.1.call-done = bf16[2048,1,1280]{2,0,1:T(8,128)(2,1)} async-done(((bf16[16,1,1280]{2,0,1:T(8,128)(2,1)}), bf16[2048,1,1280]{2,0,1:T(8,128)(2,1)}) %all-gather.5.cloned.1.call-update) | async-done | bytes 5242896 | tf_op jit(solution)/shard_map/all_gather | solution.py:178
  160.7 3.6 %multiply_reduce_fusion = f32[2048]{0:T(1024)S(1)} fusion(bf16[2048,1,1280]{2,0,1:T(8,128)(2,1)} %all-gather.5.cloned.1.call-done), kind=kLoop, calls=%fused_computation | loop fusion | flops 7862272 | bytes 5251072 | tf_op jit(solution)/shard_map/reduce_sum | solution.py:184
  164.3 0.1 reduce_sum.27
  164.5 0.1 sqrt.20
  164.6 7.3 %convert_element_type.69 = f32[2048,1,1280]{2,0,1:T(8,128)} convert(bf16[2048,1,1280]{2,0,1:T(8,128)(2,1)} %all-gather.5.cloned.1.call-done) | non-fusion elementwise | flops 2621440 | bytes 15728640 | tf_op jit(solution)/shard_map/convert_element_type | solution.py:182
  171.9 16.7 %copy.23 = f32[32,16,4,1280]{3,2,1,0:T(4,128)} copy(f32[32,16,4,1280]{3,1,2,0:T(8,128)} %bitcast.27) | data formatting | bytes 20971520 | tf_op jit(solution)/shard_map/convert_element_type | solution.py:182
  188.5 6.5 %copy.25 = f32[64,8,4,1280]{3,1,2,0:T(8,128)S(1)} copy(f32[64,8,4,1280]{3,2,1,0:T(4,128)} %bitcast.28) | data formatting | bytes 20971520
  195.0 0.6 dynamic_slice.11
  195.6 7.4 %fusion.9 = (f32[512]{0:T(512)S(1)}, f32[512,594]{0,1:T(8,128)}) fusion(bf16[5120,594]{0,1:T(8,128)(2,1)} %param.19, f32[512,5120]{1,0:T(8,128)S(1)} %bitcast.30, f32[5120]{0:T(1024)S(1)} %copy-done.3, f32[512]{0:T(512)S(1)} %sqrt.20), kind=kOutput, calls=%fused_computation.25 | convolution fusion | flops 3122438656 | bytes 17809408 | tf_op jit(solution)/shard_map/dot_general | solution.py:187
  203.0 55.1 %all-gather.2 = f32[128,1,512]{2,1,0:T(1,128)S(1)} all-gather(f32[1,1,512]{2,1,0:T(1,128)S(1)} %bitcast.34), channel_id=3, replica_groups=mesh['req'=32,'tp'=4] {'req','tp'}, dimensions={0}, use_global_device_ids=true | all-gather | bytes 264192 | tf_op jit(solution)/shard_map/all_gather | solution.py:189
  258.1 0.8 reduce_max.19
  (30 shorter events, 0.2 us)
Async XLA Ops:
  7.2 8.7 %copy-start = (bf16[5120,256]{1,0:T(8,128)(2,1)S(1)}, bf16[5120,256]{1,0:T(8,128)(2,1)}, u32[]{:S(2)}) copy-start(bf16[5120,256]{1,0:T(8,128)(2,1)} %param.14) | copy-start | bytes 7864324
  7.2 82.4 %reduce-scatter.2.cloned.1.call-start = ((), (), s32[]{:S(2)}) async-start(), calls=%async_computation.1 | async-start | bytes 4915200 | tf_op jit(solution)/shard_map/reduce_scatter | solution.py:172
  7.3 8.6 %copy-start.5 = (f32[256]{0:T(256)S(1)}, f32[256]{0:T(256)}, u32[]{:S(2)}) copy-start(f32[256]{0:T(256)} %param.15) | copy-start | bytes 3076
  11.5 5.6 %slice-start = ((s8[6553600]{0:T(1024)(128)(4,1)}), s8[2359296]{0:T(1024)(128)(4,1)S(1)}, s32[]{:S(2)}) async-start(s8[6553600]{0:T(1024)(128)(4,1)} %bitcast.35), calls=%async_computation.3 | async-start | bytes 4718592
  12.3 4.9 %slice-start.1 = ((s8[6553600]{0:T(1024)(128)(4,1)}), s8[4194304]{0:T(1024)(128)(4,1)S(1)}, s32[]{:S(2)}) async-start(s8[6553600]{0:T(1024)(128)(4,1)} %bitcast.35), calls=%async_computation.4 | async-start | bytes 8388608
  12.3 4.9 %copy-start.4 = (f32[640]{0:T(1024)S(1)}, f32[640]{0:T(1024)}, u32[]{:S(2)}) copy-start(f32[640]{0:T(1024)} %param.13) | copy-start | bytes 7684
  20.4 12.8 %slice-start.2 = ((s8[6553600]{0:T(1024)(128)(4,1)}), s8[4194304]{0:T(1024)(128)(4,1)S(1)}, s32[]{:S(2)}) async-start(s8[6553600]{0:T(1024)(128)(4,1)} %bitcast.37), calls=%async_computation.5 | async-start | bytes 8388608
  20.6 12.6 %slice-start.3 = ((s8[6553600]{0:T(1024)(128)(4,1)}), s8[2359296]{0:T(1024)(128)(4,1)S(1)}, s32[]{:S(2)}) async-start(s8[6553600]{0:T(1024)(128)(4,1)} %bitcast.37), calls=%async_computation.6 | async-start | bytes 4718592
  38.0 122.8 %all-gather.5.cloned.1.call-start = ((), (), s32[]{:S(2)}) async-start(), calls=%async_computation.2 | async-start | bytes 5283840 | tf_op jit(solution)/shard_map/all_gather | solution.py:178
  91.3 80.6 %copy-start.2 = (bf16[384,1280]{1,0:T(8,128)(2,1)}, bf16[384,1280]{1,0:T(8,128)(2,1)S(1)}, u32[]{:S(2)}) copy-start(bf16[384,1280]{1,0:T(8,128)(2,1)S(1)} %add_convert_fusion) | copy-start | bytes 2949124
  188.5 7.1 %copy-start.3 = (f32[5120]{0:T(1024)S(1)}, f32[5120]{0:T(1024)}, u32[]{:S(2)}) copy-start(f32[5120]{0:T(1024)} %param.18) | copy-start | bytes 61444
  195.6 63.3 %copy-start.1 = (bf16[5120,256]{1,0:T(8,128)(2,1)S(1)}, bf16[5120,256]{1,0:T(8,128)(2,1)}, u32[]{:S(2)}) copy-start(bf16[5120,256]{1,0:T(8,128)(2,1)} %param.14) | copy-start | bytes 7864324
Sparse Core Ops, SparseCore 0:
  38.1 51.4 reduce-scatter.1
  93.1 67.6 all-gather.4
